TPU v7x, 32 devices: a whole 2x2x4 slice. The times are simulated.
32 devices in a mesh: row: 4 (over y, x), col: 8 (over z, core).
Axes of the slice: x: 2, y: 2, z: 4, core: 2. Of those that a mesh axis runs over, the one named last changes fastest.
Arguments:
- a_terms: float32 [256, 16384], P('col', 'row'), may hold values from -6 to 6
- b_eval: float32 [512, 32768], P('col'), may hold values from -0.375 to 0.375
- term_slot: int32 [256], replicated, may hold values from 0 to 511, as said below
- term_sign: int32 [256], replicated, may hold values from -1 to 1, as said below
Outputs:
- joint: float32 [16384, 32768], P('row', 'col')
Inputs may be any that keep to these rules, and one draw needn't show every extreme that they name: `term_slot`: entries are distinct. Slot s belongs to the evaluating device s // 64 along col. The numbers of terms held by devices d and d + 4 along col sum to exactly 64 for every d under 8 // 2; in every draw one device holds exactly 64, and slots 0 and 511 are always used. Rows of b_eval at slots that no term names are not used. `term_sign`: each entry is -1 or +1.
All inputs are finite; a program needn't handle non-finite values.
Results may differ from a plain program's by a relative error of at most 0.000071.
Values sent between devices are 32-bit elements; how exact they have to be, the bound alone decides.
No kernel may reach another device: no remote copies, remote signals or barrier semaphores. Data moves between devices by JAX's collectives and lax.ppermute only.
A program may use at most 192 MiB of HBM per device.

v0:
```python
import jax
import jax.numpy as jnp
from jax import lax
from jax.sharding import PartitionSpec as P


def contract(left, right):
    return lax.dot_general(
        left,
        right,
        (((0,), (0,)), ((), ())),
        precision=lax.Precision.HIGHEST,
        preferred_element_type=jnp.float32,
    )


def shards(a_terms, b_eval, term_slot, term_sign):
    b_slots = lax.all_to_all(b_eval, "col", split_axis=1, concat_axis=0, tiled=True)
    signed = jnp.take(b_slots, term_slot, axis=0) * term_sign.astype(jnp.float32)[:, None]
    a_whole = lax.all_gather(a_terms, "col", axis=0, tiled=True)
    joint = contract(a_whole, signed)
    return joint


def solution(mesh):
    return jax.shard_map(
        shards,
        mesh=mesh,
        in_specs=(P("col", "row"), P("col", None), P(), P()),
        out_specs=P("row", "col"),
        check_vma=False,
    )
```

profile of v0, /device:TPU:0, one launch (start us, length us, event | category | flops | bytes accessed | tf_op | source)
XLA Modules:
  0.0 380.5 jit_solution(8375967575387594960)
XLA Ops:
  6.5 7.8 %copy.9 = f32[8,8,8,4096]{3,2,0,1:T(8,128)} copy(f32[8,8,8,4096]{3,2,1,0:T(8,128)} %bitcast.13) | data formatting | bytes 16777216 | tf_op jit(solution)/shard_map/all_to_all | solution.py:18
  14.3 0.0 copy-start
  14.3 0.0 copy-start.1
  14.3 6.5 %all-to-all-start = ((f32[64,8,4096]{2,0,1:T(8,128)}), f32[64,8,4096]{2,0,1:T(8,128)}, u32[]{:S(2)}, u32[]{:S(2)}) async-start(f32[64,8,4096]{2,0,1:T(8,128)} %bitcast.12), calls=%async_computation | async-start | bytes 16777216 | tf_op jit(solution)/shard_map/all_to_all | solution.py:18
  20.8 0.0 all-gather.2.cloned.1.call-start
  20.8 0.7 all-gather.2.cloned.1.call-update
  21.5 0.0 copy-done
  21.5 0.0 copy-done.1
  21.6 216.9 %all-to-all-done = f32[64,8,4096]{2,0,1:T(8,128)} async-done(((f32[64,8,4096]{2,0,1:T(8,128)}), f32[64,8,4096]{2,0,1:T(8,128)}, u32[]{:S(2)}, u32[]{:S(2)}) %all-to-all-start) | async-done | bytes 8388640 | tf_op jit(solution)/shard_map/all_to_all | solution.py:18
  238.5 9.1 %gather_fusion = f32[256,4096]{1,0:T(8,128)} fusion(f32[512,4096]{1,0:T(8,128)} %bitcast.1, s32[1024]{0:T(1024)S(1)} %pad_clamp_fusion), kind=kCustom, calls=%fused_computation | custom fusion | bytes 8389632 | tf_op jit(solution)/shard_map/jit(_take)/gather | solution.py:19
  247.6 0.0 all-gather.2.cloned.1.call-done
  247.6 60.4 %convolution_bitcast_fusion = f32[4096,4096]{0,1:T(8,128)} fusion(f32[256,4096]{1,0:T(8,128)} %all-gather.2.cloned.1.call-done, f32[256,4096]{1,0:T(8,128)} %gather_fusion, f32[256]{0:T(256)S(1)} %convert_element_type.3, pred[256]{0:T(512)(128)(4,1)S(1)} %compare_and_fusion), kind=kOutput, calls=%fused_computation.1 | convolution fusion | flops 51541704704 | bytes 75498752 | tf_op jit(solution)/shard_map/dot_general | solution.py:8
  307.9 65.7 %copy.6 = f32[4096,4096]{1,0:T(8,128)} copy(f32[4096,4096]{0,1:T(8,128)} %convolution_bitcast_fusion) | data formatting | bytes 134217728 | tf_op jit(solution)/shard_map/dot_general | solution.py:8
  (4 shorter events, 0.0 us)
Async XLA Ops:
  14.3 7.2 %copy-start = (s32[256]{0:T(256)S(1)}, s32[256]{0:T(256)}, u32[]{:S(2)}) copy-start(s32[256]{0:T(256)} %param.7) | copy-start | bytes 3076
  14.3 7.2 %copy-start.1 = (s32[256]{0:T(256)S(1)}, s32[256]{0:T(256)}, u32[]{:S(2)}) copy-start(s32[256]{0:T(256)} %param.6) | copy-start | bytes 3076
  14.3 224.2 %all-to-all-start = ((f32[64,8,4096]{2,0,1:T(8,128)}), f32[64,8,4096]{2,0,1:T(8,128)}, u32[]{:S(2)}, u32[]{:S(2)}) async-start(f32[64,8,4096]{2,0,1:T(8,128)} %bitcast.12), calls=%async_computation | async-start | bytes 16777216 | tf_op jit(solution)/shard_map/all_to_all | solution.py:18
  20.8 226.8 %all-gather.2.cloned.1.call-start = ((), (), s32[]{:S(2)}) async-start(), calls=%async_computation.1 | async-start | bytes 4718592 | tf_op jit(solution)/shard_map/all_gather | solution.py:20
Sparse Core Ops, SparseCore 0:
  23.2 85.1 all-gather.1
where the time goes:
time: 382 us; the launch traced here: 381 us
  waiting for transfers between devices  218 us (57%)
  local copies, waits for them, and re-layouts  82.6 us (22%)
  matrix products  60.4 us (16%)
  between operations  13.4 us (4%)
  starting transfers between devices  6.49 us (2%)
    all_to_all x1, waiting for transfers between devices, shards(): lax.all_to_all(b_eval, 'col', split_axis=1, concat_axis=0, tiled=True)  217 us
    dot_general x1, local copies, waits for them, and re-layouts, contract(): lax.dot_general(left, right, (((0,), (0,)), ((), ())), precision=lax.Prec...  65.7 us
    dot_general x1, matrix products, contract(): lax.dot_general(left, right, (((0,), (0,)), ((), ())), precision=lax.Prec...  60.4 us
    gather x1, local copies, waits for them, and re-layouts, shards(): jnp.take(b_slots, term_slot, axis=0)  9.08 us
    all_to_all x1, local copies, waits for them, and re-layouts, shards(): lax.all_to_all(b_eval, 'col', split_axis=1, concat_axis=0, tiled=True)  7.77 us
  transfers between devices with their start and end apart: 2, of which 1 were waited for; matrix products, arithmetic and copies ran while one was open for 2% of the time, Pallas kernels for 0%

commit v1 on v0

v1 whole, which is shorter than its diff:
```python
import jax
import jax.numpy as jnp
from jax import lax
from jax.sharding import PartitionSpec as P


def contract(left, right):
    return lax.dot_general(
        left,
        right,
        (((0,), (0,)), ((), ())),
        precision=lax.Precision.HIGH,
        preferred_element_type=jnp.float32,
    )


def solution(mesh):
    rows, cols = mesh.shape["row"], mesh.shape["col"]

    def shards(a_terms, b_eval, term_slot, term_sign):
        slots = b_eval.shape[0]
        part = b_eval.shape[1] // (rows * cols)
        mine = lax.dynamic_index_in_dim(b_eval.reshape(slots, cols, rows, part), lax.axis_index("row"), 2, keepdims=False)
        b_slots = lax.all_to_all(mine.transpose(1, 0, 2), "col", split_axis=0, concat_axis=0, tiled=True)
        b_slots = b_slots.reshape(cols * slots, part)
        signed = jnp.take(b_slots, term_slot, axis=0) * term_sign.astype(jnp.float32)[:, None]
        signed = lax.all_gather(signed, "row", axis=1, tiled=True)
        a_whole = lax.all_gather(a_terms, "col", axis=0, tiled=True)
        return contract(a_whole, signed)

    return jax.shard_map(
        shards,
        mesh=mesh,
        in_specs=(P("col", "row"), P("col", None), P(), P()),
        out_specs=P("row", "col"),
        check_vma=False,
    )
```

time: 382 us -> 265 us (0.69)
  waiting for transfers between devices: 218 us -> 121 us
  matrix products: 60.4 us -> 35.3 us
    all_to_all x1, waiting for transfers between devices: 217 us -> 68.8 us  [shards(): lax.all_to_all(mine.transpose(1, 0, 2), 'col', split_axis=0, concat_axis=...]
    all_gather x0 -> x1, waiting for transfers between devices: none -> 51.5 us  [shards(): signed = lax.all_gather(signed, 'row', axis=1, tiled=True)]
    dot_general x1, matrix products: 60.4 us -> 35.3 us  [contract(): lax.dot_general(left, right, (((0,), (0,)), ((), ())), precision=lax.Prec...]
    reshape x0 -> x1, local copies, waits for them, and re-layouts: none -> 10.8 us  [shards(): b_eval.reshape(slots, cols, rows, part)]
    dynamic_slice x0 -> x2, local copies, waits for them, and re-layouts: none -> 8.73 us  [shards(): lax.dynamic_index_in_dim(b_eval.reshape(slots, cols, rows, part), lax.axi...]
    gather x1, local copies, waits for them, and re-layouts: 9.08 us -> 1.07 us  [shards(): jnp.take(b_slots, term_slot, axis=0)]
    all_to_all x1 -> x0, local copies, waits for them, and re-layouts: 7.77 us -> none  [shards(): lax.all_to_all(b_eval, 'col', split_axis=1, concat_axis=0, tiled=True)]
  transfers between devices with their start and end apart: 2 -> 3, of which waited for: 1 -> 2; matrix products, arithmetic and copies ran while one was open for 2% -> 8% of each run, Pallas kernels for 0% -> 0%
where the time goes in v1:
time: 265 us; the launch traced here: 264 us
  waiting for transfers between devices  121 us (46%)
  local copies, waits for them, and re-layouts  86.4 us (33%)
  matrix products  35.3 us (13%)
  between operations  13.5 us (5%)
  starting transfers between devices  6.34 us (2%)
    all_to_all x1, waiting for transfers between devices, shards(): lax.all_to_all(mine.transpose(1, 0, 2), 'col', split_axis=0, concat_axis=...  68.8 us
    dot_general x1, local copies, waits for them, and re-layouts, contract(): lax.dot_general(left, right, (((0,), (0,)), ((), ())), precision=lax.Prec...  65.7 us
    all_gather x1, waiting for transfers between devices, shards(): signed = lax.all_gather(signed, 'row', axis=1, tiled=True)  51.5 us
    dot_general x1, matrix products, contract(): lax.dot_general(left, right, (((0,), (0,)), ((), ())), precision=lax.Prec...  35.3 us
    reshape x1, local copies, waits for them, and re-layouts, shards(): b_eval.reshape(slots, cols, rows, part)  10.8 us
    dynamic_slice x2, local copies, waits for them, and re-layouts, shards(): lax.dynamic_index_in_dim(b_eval.reshape(slots, cols, rows, part), lax.axi...  8.73 us
    all_to_all x1, starting transfers between devices, shards(): lax.all_to_all(mine.transpose(1, 0, 2), 'col', split_axis=0, concat_axis=...  6.12 us
  transfers between devices with their start and end apart: 3, of which 2 were waited for; matrix products, arithmetic and copies ran while one was open for 8% of the time, Pallas kernels for 0%

profile of v1, /device:TPU:0, one launch (start us, length us, event | category | flops | bytes accessed | tf_op | source)
XLA Modules:
  0.0 263.8 jit_solution(10862979123758307668)
XLA Ops:
  6.5 0.0 all-gather.5.cloned.1.call-start
  6.5 0.7 all-gather.5.cloned.1.call-update
  7.3 10.8 %reshape.12 = f32[64,8,4,1024]{3,2,1,0:T(4,128)} reshape(f32[64,32768]{1,0:T(8,128)} %param.5) | data formatting | bytes 16777216 | tf_op jit(solution)/shard_map/reshape | solution.py:23
  18.1 6.2 %constant_dynamic-slice_fusion = f32[64,8,1,1024]{3,2,1,0:T(1,128)S(1)} fusion(f32[64,8,4,1024]{3,2,1,0:T(4,128)} %reshape.12, s32[]{:T(128)S(6)} %select_n.14), kind=kLoop, calls=%fused_computation.7 | loop fusion | bytes 4194308 | tf_op jit(solution)/shard_map/jit(dynamic_index_in_dim)/dynamic_slice | solution.py:23
  24.3 0.0 copy-start
  24.3 0.0 copy-start.1
  24.3 2.5 copy.8
  26.9 6.1 %all-to-all-start = ((f32[8,64,1024]{2,1,0:T(8,128)}), f32[8,64,1024]{2,1,0:T(8,128)S(1)}, u32[]{:S(2)}, u32[]{:S(2)}) async-start(f32[8,64,1024]{2,1,0:T(8,128)} %bitcast.11), calls=%async_computation | async-start | bytes 4194304 | tf_op jit(solution)/shard_map/all_to_all | solution.py:24
  33.0 0.2 all-gather.3.cloned.1.call-start
  33.2 0.0 copy-done
  33.2 0.0 copy-done.1
  33.3 68.8 %all-to-all-done = f32[8,64,1024]{2,1,0:T(8,128)S(1)} async-done(((f32[8,64,1024]{2,1,0:T(8,128)}), f32[8,64,1024]{2,1,0:T(8,128)S(1)}, u32[]{:S(2)}, u32[]{:S(2)}) %all-to-all-start) | async-done | bytes 2097184 | tf_op jit(solution)/shard_map/all_to_all | solution.py:24
  102.1 1.1 gather_fusion
  103.1 1.1 select_multiply_fusion
  104.3 0.0 all-gather.3.cloned.1.call-update
  104.3 0.0 all-gather.5.cloned.1.call-done
  104.3 51.5 %all-gather.3.cloned.1.call-done = f32[256,4096]{1,0:T(8,128)} async-done(((f32[256,1024]{1,0:T(8,128)}), f32[256,4096]{1,0:T(8,128)}) %all-gather.3.cloned.1.call-update) | async-done | bytes 4194320 | tf_op jit(solution)/shard_map/all_gather | solution.py:27
  155.9 35.3 %convolution_bitcast_fusion = f32[4096,4096]{0,1:T(8,128)} fusion(f32[256,4096]{1,0:T(8,128)} %all-gather.3.cloned.1.call-done, f32[256,4096]{1,0:T(8,128)} %all-gather.5.cloned.1.call-done), kind=kOutput, calls=%fused_computation.1 | convolution fusion | flops 25769803776 | bytes 75497472 | tf_op jit(solution)/shard_map/dot_general | solution.py:8
  191.2 65.7 %copy.6 = f32[4096,4096]{1,0:T(8,128)} copy(f32[4096,4096]{0,1:T(8,128)} %convolution_bitcast_fusion) | data formatting | bytes 134217728 | tf_op jit(solution)/shard_map/dot_general | solution.py:8
  (4 shorter events, 0.0 us)
Async XLA Ops:
  6.5 97.8 %all-gather.5.cloned.1.call-start = ((), (), s32[]{:S(2)}) async-start(), calls=%async_computation.2 | async-start | bytes 4718592 | tf_op jit(solution)/shard_map/all_gather | solution.py:28
  24.3 8.9 %copy-start = (s32[256]{0:T(256)S(1)}, s32[256]{0:T(256)}, u32[]{:S(2)}) copy-start(s32[256]{0:T(256)} %param.7) | copy-start | bytes 3076
  24.3 8.9 %copy-start.1 = (s32[256]{0:T(256)S(1)}, s32[256]{0:T(256)}, u32[]{:S(2)}) copy-start(s32[256]{0:T(256)} %param.6) | copy-start | bytes 3076
  26.9 75.2 %all-to-all-start = ((f32[8,64,1024]{2,1,0:T(8,128)}), f32[8,64,1024]{2,1,0:T(8,128)S(1)}, u32[]{:S(2)}, u32[]{:S(2)}) async-start(f32[8,64,1024]{2,1,0:T(8,128)} %bitcast.11), calls=%async_computation | async-start | bytes 4194304 | tf_op jit(solution)/shard_map/all_to_all | solution.py:24
  33.0 122.9 %all-gather.3.cloned.1.call-start = ((), (), s32[]{:S(2)}) async-start(), calls=%async_computation.1 | async-start | bytes 5242880 | tf_op jit(solution)/shard_map/all_gather | solution.py:27
Sparse Core Ops, SparseCore 0:
  9.0 69.5 all-gather.4
  104.4 51.4 all-gather.2

commit v2 on v1

v2 whole, which is shorter than its diff:
```python
import jax
import jax.numpy as jnp
from jax import lax
from jax.experimental import pallas as pl
from jax.experimental.pallas import tpu as pltpu
from jax.sharding import PartitionSpec as P

BF16, F32 = jnp.bfloat16, jnp.float32
VMEM_BYTES = 48 << 20


def halves(x):
    high = x.astype(BF16)
    return high, (x - high.astype(F32)).astype(BF16)


def dot(left, right):
    return jnp.dot(left, right, preferred_element_type=F32)


def cost(flops, moved):
    return pl.CostEstimate(flops=flops, bytes_accessed=moved, transcendentals=0)


def cut_blocks(b_eval, starts, widths):
    slots, cols = b_eval.shape[0], starts.shape[0]
    shapes = [jax.ShapeDtypeStruct((cols, slots, w), F32) for w in widths]

    def kernel(starts_ref, b_ref, *refs):
        outs, sems = refs[:-1], refs[-1]
        copies = []
        offset = 0
        for chunk, w in enumerate(widths):
            for q in range(cols):
                start = pl.multiple_of(starts_ref[q] + offset, 128)
                copies.append(
                    pltpu.make_async_copy(b_ref.at[:, pl.ds(start, w)], outs[chunk].at[q], sems.at[len(copies)])
                )
            offset += w
        for copy in copies:
            copy.start()
        for copy in copies:
            copy.wait()

    return pl.pallas_call(
        kernel,
        in_specs=[pl.BlockSpec(memory_space=pltpu.SMEM), pl.BlockSpec(memory_space=pl.ANY)],
        out_specs=[pl.BlockSpec(memory_space=pltpu.VMEM)] * len(shapes),
        out_shape=shapes,
        scratch_shapes=[pltpu.SemaphoreType.DMA((len(shapes) * cols,))],
        cost_estimate=cost(0, 8 * cols * slots * sum(widths)),
        name="cut_blocks",
    )(starts, b_eval)


def pack(blocks, select, at, w):
    cols, slots, _ = blocks.shape
    terms = select.shape[0]
    tile = min(w, 256)

    def kernel(select_ref, block_ref, out_ref):
        high, low = halves(block_ref[...].reshape(cols * slots, tile))
        out_ref[...] = dot(select_ref[...], high) + dot(select_ref[...], low)

    return pl.pallas_call(
        kernel,
        grid=(w // tile,),
        in_specs=[
            pl.BlockSpec(select.shape, lambda g: (0, 0)),
            pl.BlockSpec((cols, slots, tile), lambda g: (0, 0, at // tile + g)),
        ],
        out_specs=pl.BlockSpec((terms, tile), lambda g: (0, g)),
        out_shape=jax.ShapeDtypeStruct((terms, w), F32),
        cost_estimate=cost(4 * cols * slots * w * terms, 4 * (cols * slots + terms) * w),
        name="pack",
    )(select, blocks)


def split_a(parts):
    held, bins = parts[0].shape
    terms, tile = held * len(parts), min(bins, 1024)

    def kernel(*refs):
        high_ref, low_ref = refs[len(parts) :]
        for n in range(len(parts)):
            at = slice(n * held, (n + 1) * held)
            high_ref[:, at], low_ref[:, at] = halves(refs[n][...].T)

    return pl.pallas_call(
        kernel,
        grid=(bins // tile,),
        in_specs=[pl.BlockSpec((held, tile), lambda i: (0, i))] * len(parts),
        out_specs=[pl.BlockSpec((tile, terms), lambda i: (i, 0))] * 2,
        out_shape=[jax.ShapeDtypeStruct((bins, terms), BF16)] * 2,
        compiler_params=pltpu.CompilerParams(vmem_limit_bytes=VMEM_BYTES),
        cost_estimate=cost(0, 8 * bins * terms),
        name="split_a",
    )(*parts)


def product(high, low, pieces, places, joint, columns):
    bins, terms = high.shape
    count, w = len(pieces), pieces[0].shape[1]
    tile = min(bins, (1 << 21) // w)
    fresh = joint is None

    def kernel(places_ref, high_ref, low_ref, *refs):
        out_ref, b_high, b_low = refs[-3:]

        @pl.when(pl.program_id(1) == 0)
        def _():
            for p in range(count):
                @pl.when(pl.program_id(0) == p)
                def _():
                    b_high[...], b_low[...] = halves(refs[p][...])

        a_high, a_low = high_ref[...], low_ref[...]
        out_ref[...] = dot(a_high, b_high[...]) + dot(a_high, b_low[...]) + dot(a_low, b_high[...])

    row = lambda j, i, places_ref: (i, 0)
    whole = lambda j, i, places_ref: (0, 0)
    return pl.pallas_call(
        kernel,
        grid_spec=pltpu.PrefetchScalarGridSpec(
            num_scalar_prefetch=1,
            grid=(count, bins // tile),
            in_specs=[pl.BlockSpec((tile, terms), row)] * 2
            + [pl.BlockSpec((terms, w), whole)] * count
            + ([] if fresh else [pl.BlockSpec(memory_space=pl.ANY)]),
            out_specs=pl.BlockSpec((tile, w), lambda j, i, places_ref: (i, places_ref[j])),
            scratch_shapes=[pltpu.VMEM((terms, w), BF16)] * 2,
        ),
        out_shape=jax.ShapeDtypeStruct((bins, columns), F32),
        input_output_aliases={} if fresh else {3 + count: 0},
        compiler_params=pltpu.CompilerParams(vmem_limit_bytes=VMEM_BYTES),
        cost_estimate=cost(6 * bins * terms * count * w, 4 * bins * count * w),
        name="product",
    )(places, high, low, *pieces, *([] if fresh else [joint]))


def after(values, *earlier):
    return lax.optimization_barrier((values, earlier))[0]


def solution(mesh):
    rows, cols = mesh.shape["row"], mesh.shape["col"]

    def shards(a_terms, b_eval, term_slot, term_sign):
        slots, wide = b_eval.shape
        per = wide // cols
        part = per // rows
        if rows == 4 and part % 1024 == 0:
            crossings = [[part // 2], [part // 2]]
        else:
            crossings = [[part]]
        r = lax.axis_index("row")

        starts = (jnp.arange(cols) * per + r * part).astype(jnp.int32)
        cut = cut_blocks(b_eval, starts, [sum(c) for c in crossings])
        a_whole = lax.all_gather(a_terms, "col", axis=0, tiled=True)
        used = term_slot[:, None] == jnp.arange(cols * slots)[None, :]
        select = jnp.where(used, term_sign[:, None], 0).astype(BF16)
        high, low = split_a([a_whole])

        mine, places, pieces, offset, blocks = [], [], [], 0, None
        for c, widths in enumerate(crossings):
            block = cut[c] if blocks is None else after(cut[c], blocks)
            blocks = lax.all_to_all(block, "col", 0, 0, tiled=True)
            if c and c == len(crossings) - 1:
                blocks = after(blocks, high, low)
            at = 0
            for w in widths:
                mine.append(pack(blocks, select, at, w))
                if rows == 4:
                    pieces.append([mine[-1]] + [lax.ppermute(mine[-1], "row", [(q, q ^ n) for q in range(4)]) for n in (1, 2, 3)])
                    quarter = jnp.stack([r, r ^ 1, r ^ 2, r ^ 3])
                else:
                    pieces.append(list(lax.all_gather(mine[-1], "row")))
                    quarter = jnp.arange(rows)
                places.append((quarter * (part // w) + offset // w).astype(jnp.int32))
                at, offset = at + w, offset + w
        joint = None
        for n in range(len(mine)):
            ready = pieces[n] if n == len(mine) - 1 else after(pieces[n], mine[n + 1])
            joint = product(high, low, ready, places[n], joint, per)
        return joint

    return jax.shard_map(
        shards,
        mesh=mesh,
        in_specs=(P("col", "row"), P("col", None), P(), P()),
        out_specs=P("row", "col"),
        check_vma=False,
    )
```

time: 265 us -> 157 us (0.59)
  waiting for transfers between devices: 121 us -> 17 us
  local copies, waits for them, and re-layouts: 86.4 us -> 2.38 us
  blocking collectives: 0 us -> 59.2 us
  Pallas kernels: 0 us -> 51.8 us
  matrix products: 35.3 us -> 0 us
  starting transfers between devices: 6.34 us -> 11.2 us
    dot_general x1 -> x0, local copies, waits for them, and re-layouts: 65.7 us -> none  [contract(): lax.dot_general(left, right, (((0,), (0,)), ((), ())), precision=lax.Prec...]
    all_to_all x0 -> x1, blocking collectives: none -> 59.2 us  [shards(): blocks = lax.all_to_all(block, 'col', 0, 0, tiled=True)]
    all_to_all x1, waiting for transfers between devices: 68.8 us -> 14.8 us  [shards(): blocks = lax.all_to_all(block, 'col', 0, 0, tiled=True)]
    pallas_call x0 -> x6, Pallas kernels: none -> 51.8 us  [the longest x2 39.6 us: product(): pl.pallas_call(kernel, grid_spec=pltpu.PrefetchScalarGridSpec(num_scalar_...]
    all_gather x1 -> x0, waiting for transfers between devices: 51.5 us -> none  [shards(): signed = lax.all_gather(signed, 'row', axis=1, tiled=True)]
    dot_general x1 -> x0, matrix products: 35.3 us -> none  [contract(): lax.dot_general(left, right, (((0,), (0,)), ((), ())), precision=lax.Prec...]
    reshape x1 -> x0, local copies, waits for them, and re-layouts: 10.8 us -> none  [shards(): b_eval.reshape(slots, cols, rows, part)]
    dynamic_slice x2 -> x0, local copies, waits for them, and re-layouts: 8.73 us -> none  [shards(): lax.dynamic_index_in_dim(b_eval.reshape(slots, cols, rows, part), lax.axi...]
  transfers between devices with their start and end apart: 3 -> 8, of which waited for: 2 -> 3; matrix products, arithmetic and copies ran while one was open for 8% -> 1% of each run, Pallas kernels for 0% -> 20%
where the time goes in v2:
time: 157 us
  blocking collectives  59.2 us (38%)
  Pallas kernels  51.8 us (33%)
  waiting for transfers between devices  17 us (11%)
  between operations  13.5 us (9%)
  starting transfers between devices  11.2 us (7%)
  local copies, waits for them, and re-layouts  2.38 us (2%)
    all_to_all x1, blocking collectives, shards(): blocks = lax.all_to_all(block, 'col', 0, 0, tiled=True)  59.2 us
    pallas_call x2, Pallas kernels, product(): pl.pallas_call(kernel, grid_spec=pltpu.PrefetchScalarGridSpec(num_scalar_...  39.6 us
    all_to_all x1, waiting for transfers between devices, shards(): blocks = lax.all_to_all(block, 'col', 0, 0, tiled=True)  14.8 us
    ppermute x6, starting transfers between devices, shards(): lax.ppermute(mine[-1], 'row', [(q, q ^ n) for q in range(4)])  6.98 us
    pallas_call x2, Pallas kernels, pack(): pl.pallas_call(kernel, grid=(w // tile,), in_specs=[pl.BlockSpec(select.s...  4.93 us
    all_to_all x1, starting transfers between devices, shards(): blocks = lax.all_to_all(block, 'col', 0, 0, tiled=True)  4.26 us
    pallas_call x1, Pallas kernels, cut_blocks(): pl.pallas_call(kernel, in_specs=[pl.BlockSpec(memory_space=pltpu.SMEM), p...  3.73 us
    pallas_call x1, Pallas kernels, split_a(): pl.pallas_call(kernel, grid=(bins // tile,), in_specs=[pl.BlockSpec((held...  3.59 us
  transfers between devices with their start and end apart: 8, of which 3 were waited for; matrix products, arithmetic and copies ran while one was open for 1% of the time, Pallas kernels for 20%

profile of v2, /device:TPU:0, one launch (start us, length us, event | category | flops | bytes accessed | tf_op | source)
XLA Modules:
  0.0 156.6 jit_solution(15780894075733814879)
XLA Ops:
  6.5 0.0 copy-start.3
  6.5 0.0 copy-start.4
  6.5 0.0 all-gather.2.cloned.1.call-start
  6.5 0.7 all-gather.2.cloned.1.call-update
  7.3 0.6 multiply_add_fusion.starts_ref
  7.8 3.7 %cut_blocks.1 = (f32[8,64,512]{2,1,0:T(8,128)}, f32[8,64,512]{2,1,0:T(8,128)}) custom-call(s32[8]{0:T(128)} %multiply_add_fusion.starts_ref, f32[64,32768]{1,0:T(8,128)} %b_ref.1), custom_call_target="tpu_custom_call" | custom-call | bytes 4194304 | tf_op jit(solution)/shard_map/cut_blocks/pallas_call | solution.py:45
  11.6 59.2 %all_to_all.10.block_ref = f32[8,64,512]{2,1,0:T(8,128)} all-to-all(f32[8,64,512]{2,1,0:T(8,128)} %get-tuple-element.18), channel_id=1, replica_groups=mesh['row'=4,'col'=8] {'col'}, dimensions={0} | all-to-all | bytes 2097152 | tf_op jit(solution)/shard_map/all_to_all | solution.py:168
  70.8 4.3 %all-to-all-start.1 = ((f32[8,64,512]{2,1,0:T(8,128)}), f32[8,64,512]{2,1,0:T(8,128)}, u32[]{:S(2)}, u32[]{:S(2)}) async-start(f32[8,64,512]{2,1,0:T(8,128)} %get-tuple-element.19), calls=%async_computation.1 | async-start | bytes 2097152 | tf_op jit(solution)/shard_map/all_to_all | solution.py:168
  75.1 0.0 copy-done.3
  75.1 0.0 copy-done.4
  75.1 0.8 select_convert_fusion.select_ref
  75.9 2.5 %pack.3.refs_0_ = f32[256,512]{1,0:T(8,128)} custom-call(bf16[256,512]{1,0:T(8,128)(2,1)} %select_convert_fusion.select_ref, f32[8,64,512]{2,1,0:T(8,128)} %all_to_all.10.block_ref), custom_call_target="tpu_custom_call" | custom-call | flops 268435456 | bytes 1572864 | tf_op jit(solution)/shard_map/pack/pallas_call | solution.py:65
  78.4 2.4 %collective-permute-start.5 = (f32[256,512]{1,0:T(8,128)}, f32[256,512]{1,0:T(8,128)S(1)}, u32[]{:S(2)}, u32[]{:S(2)}) collective-permute-start(f32[256,512]{1,0:T(8,128)} %pack.3.refs_0_), channel_id=1, source_target_pairs={{0,24},{8,16},{16,8},{24,0},{1,25},{9,17},{17,9},{25,1},{2,26},{10... | collective-permute-start | bytes 1572872 | tf_op jit(solution)/shard_map/ppermute | solution.py:175
  80.8 0.5 collective-permute-start.4
  81.3 0.6 collective-permute-start.3
  81.9 0.1 broadcast_add_fusion
  82.0 0.0 all-gather.2.cloned.1.call-done.refs_0_
  82.0 3.6 %split_a.1 = (bf16[4096,256]{1,0:T(8,128)(2,1)S(1)}, bf16[4096,256]{1,0:T(8,128)(2,1)S(1)}) custom-call(f32[256,4096]{1,0:T(8,128)} %all-gather.2.cloned.1.call-done.refs_0_), custom_call_target="tpu_custom_call" | custom-call | bytes 8388608 | tf_op jit(solution)/shard_map/split_a/pallas_call | solution.py:89
  85.6 0.0 copy-start
  85.6 1.3 copy-done
  86.9 14.8 %all-to-all-done.1.block_ref = f32[8,64,512]{2,1,0:T(8,128)} async-done(((f32[8,64,512]{2,1,0:T(8,128)}), f32[8,64,512]{2,1,0:T(8,128)}, u32[]{:S(2)}, u32[]{:S(2)}) %all-to-all-start.1) | async-done | bytes 1048608 | tf_op jit(solution)/shard_map/all_to_all | solution.py:168
  101.7 2.5 %pack.2.refs_0_ = f32[256,512]{1,0:T(8,128)} custom-call(bf16[256,512]{1,0:T(8,128)(2,1)} %select_convert_fusion.select_ref, f32[8,64,512]{2,1,0:T(8,128)} %all-to-all-done.1.block_ref), custom_call_target="tpu_custom_call" | custom-call | flops 268435456 | bytes 1572864 | tf_op jit(solution)/shard_map/pack/pallas_call | solution.py:65
  104.1 2.4 %collective-permute-start.2 = (f32[256,512]{1,0:T(8,128)}, f32[256,512]{1,0:T(8,128)S(1)}, u32[]{:S(2)}, u32[]{:S(2)}) collective-permute-start(f32[256,512]{1,0:T(8,128)} %pack.2.refs_0_), channel_id=1, source_target_pairs={{0,24},{8,16},{16,8},{24,0},{1,25},{9,17},{17,9},{25,1},{2,26},{10... | collective-permute-start | bytes 1572872 | tf_op jit(solution)/shard_map/ppermute | solution.py:175
  106.5 0.5 collective-permute-start.1
  107.0 0.0 collective-permute-done.5.refs_3_
  107.0 0.6 collective-permute-start
  107.6 0.0 collective-permute-done.4.refs_2_
  107.6 0.0 collective-permute-done.3.refs_1_
  107.6 0.0 copy-start.1
  107.6 1.0 copy-done.1
  108.7 0.0 copy-start.2
  108.7 19.8 %product.2.refs_4_ = f32[4096,4096]{1,0:T(8,128)} custom-call(s32[4]{0:T(128)S(1)} %get-tuple-element.26.places_ref, bf16[4096,256]{1,0:T(8,128)(2,1)S(1)} %get-tuple-element.15.high_ref, bf16[4096,256]{1,0:T(8,128)(2,1)} %copy-done, f32[256,512]{1,0:T(8,128)S(1)} %copy-done.1, f32[256,512]{1,0:T(8,128)} %collective-permute-done.3.refs_1_, ...), custom_call_target="tpu_custom_call" | custom-call | flops 12884901888 | bytes 33554432 | tf_op jit(solution)/shard_map/product/pallas_call | solution.py:122
  128.5 0.0 collective-permute-done.2.refs_3_
  128.5 1.4 collective-permute-done.1.refs_2_
  129.9 0.1 collective-permute-done.refs_1_
  130.0 0.0 copy-done.2
  130.0 19.8 %product.3 = f32[4096,4096]{1,0:T(8,128)} custom-call(s32[4]{0:T(128)S(1)} %get-tuple-element.25.places_ref, bf16[4096,256]{1,0:T(8,128)(2,1)S(1)} %get-tuple-element.15.high_ref, bf16[4096,256]{1,0:T(8,128)(2,1)} %copy-done, f32[256,512]{1,0:T(8,128)S(1)} %copy-done.2, f32[256,512]{1,0:T(8,128)S(1)} %collective-permute-done.refs_1_, ...), custom_call_target="tpu_custom_call", output_to_operand_aliasing={{}: (7, {})} | custom-call | flops 12884901888 | bytes 33554432 | tf_op jit(solution)/shard_map/product/pallas_call | solution.py:122
Async XLA Ops:
  6.5 68.5 %copy-start.3 = (s32[256]{0:T(256)S(1)}, s32[256]{0:T(256)}, u32[]{:S(2)}) copy-start(s32[256]{0:T(256)} %param.7) | copy-start | bytes 3076
  6.5 68.6 %copy-start.4 = (s32[256]{0:T(256)S(1)}, s32[256]{0:T(256)}, u32[]{:S(2)}) copy-start(s32[256]{0:T(256)} %param.6) | copy-start | bytes 3076
  6.5 75.4 %all-gather.2.cloned.1.call-start = ((), (), s32[]{:S(2)}) async-start(), calls=%async_computation.2 | async-start | bytes 4718592 | tf_op jit(solution)/shard_map/all_gather | solution.py:160
  70.8 30.9 %all-to-all-start.1 = ((f32[8,64,512]{2,1,0:T(8,128)}), f32[8,64,512]{2,1,0:T(8,128)}, u32[]{:S(2)}, u32[]{:S(2)}) async-start(f32[8,64,512]{2,1,0:T(8,128)} %get-tuple-element.19), calls=%async_computation.1 | async-start | bytes 2097152 | tf_op jit(solution)/shard_map/all_to_all | solution.py:168
  78.4 28.6 %collective-permute-start.5 = (f32[256,512]{1,0:T(8,128)}, f32[256,512]{1,0:T(8,128)S(1)}, u32[]{:S(2)}, u32[]{:S(2)}) collective-permute-start(f32[256,512]{1,0:T(8,128)} %pack.3.refs_0_), channel_id=1, source_target_pairs={{0,24},{8,16},{16,8},{24,0},{1,25},{9,17},{17,9},{25,1},{2,26},{10... | collective-permute-start | bytes 1572872 | tf_op jit(solution)/shard_map/ppermute | solution.py:175
  80.8 26.8 %collective-permute-start.4 = (f32[256,512]{1,0:T(8,128)}, f32[256,512]{1,0:T(8,128)S(1)}, u32[]{:S(2)}, u32[]{:S(2)}) collective-permute-start(f32[256,512]{1,0:T(8,128)} %pack.3.refs_0_), channel_id=1, source_target_pairs={{0,16},{8,24},{16,0},{24,8},{1,17},{9,25},{17,1},{25,9},{2,18},{10... | collective-permute-start | bytes 1572872 | tf_op jit(solution)/shard_map/ppermute | solution.py:175
  81.3 26.3 %collective-permute-start.3 = (f32[256,512]{1,0:T(8,128)}, f32[256,512]{1,0:T(8,128)}, u32[]{:S(2)}, u32[]{:S(2)}) collective-permute-start(f32[256,512]{1,0:T(8,128)} %pack.3.refs_0_), channel_id=1, source_target_pairs={{0,8},{8,0},{16,24},{24,16},{1,9},{9,1},{17,25},{25,17},{2,10},{10... | collective-permute-start | bytes 1572872 | tf_op jit(solution)/shard_map/ppermute | solution.py:175
  85.6 1.3 copy-start
  104.1 24.4 %collective-permute-start.2 = (f32[256,512]{1,0:T(8,128)}, f32[256,512]{1,0:T(8,128)S(1)}, u32[]{:S(2)}, u32[]{:S(2)}) collective-permute-start(f32[256,512]{1,0:T(8,128)} %pack.2.refs_0_), channel_id=1, source_target_pairs={{0,24},{8,16},{16,8},{24,0},{1,25},{9,17},{17,9},{25,1},{2,26},{10... | collective-permute-start | bytes 1572872 | tf_op jit(solution)/shard_map/ppermute | solution.py:175
  106.5 23.4 %collective-permute-start.1 = (f32[256,512]{1,0:T(8,128)}, f32[256,512]{1,0:T(8,128)S(1)}, u32[]{:S(2)}, u32[]{:S(2)}) collective-permute-start(f32[256,512]{1,0:T(8,128)} %pack.2.refs_0_), channel_id=1, source_target_pairs={{0,16},{8,24},{16,0},{24,8},{1,17},{9,25},{17,1},{25,9},{2,18},{10... | collective-permute-start | bytes 1572872 | tf_op jit(solution)/shard_map/ppermute | solution.py:175
  107.0 23.0 %collective-permute-start = (f32[256,512]{1,0:T(8,128)}, f32[256,512]{1,0:T(8,128)S(1)}, u32[]{:S(2)}, u32[]{:S(2)}) collective-permute-start(f32[256,512]{1,0:T(8,128)} %pack.2.refs_0_), channel_id=1, source_target_pairs={{0,8},{8,0},{16,24},{24,16},{1,9},{9,1},{17,25},{25,17},{2,10},{10... | collective-permute-start | bytes 1572872 | tf_op jit(solution)/shard_map/ppermute | solution.py:175
  107.6 1.0 copy-start.1
  108.7 21.3 %copy-start.2 = (f32[256,512]{1,0:T(8,128)S(1)}, f32[256,512]{1,0:T(8,128)}, u32[]{:S(2)}) copy-start(f32[256,512]{1,0:T(8,128)} %pack.2.refs_0_) | copy-start | bytes 1572868
Sparse Core Ops, SparseCore 0:
  9.0 70.8 all-gather.1

commit v3 on v2

--- a/solution.py
+++ b/solution.py
@@ -22,17 +22,18 @@
     return pl.CostEstimate(flops=flops, bytes_accessed=moved, transcendentals=0)
 
 
-def cut_blocks(b_eval, starts, widths):
-    slots, cols = b_eval.shape[0], starts.shape[0]
+def cut_blocks(b_eval, cols, rows, widths):
+    slots, per = b_eval.shape[0], b_eval.shape[1] // cols
     shapes = [jax.ShapeDtypeStruct((cols, slots, w), F32) for w in widths]
 
-    def kernel(starts_ref, b_ref, *refs):
+    def kernel(b_ref, *refs):
+        mine = lax.axis_index("row") * (per // rows)
         outs, sems = refs[:-1], refs[-1]
         copies = []
         offset = 0
         for chunk, w in enumerate(widths):
             for q in range(cols):
-                start = pl.multiple_of(starts_ref[q] + offset, 128)
+                start = pl.multiple_of(mine + (q * per + offset), 128)
                 copies.append(
                     pltpu.make_async_copy(b_ref.at[:, pl.ds(start, w)], outs[chunk].at[q], sems.at[len(copies)])
                 )
@@ -44,13 +45,13 @@
 
     return pl.pallas_call(
         kernel,
-        in_specs=[pl.BlockSpec(memory_space=pltpu.SMEM), pl.BlockSpec(memory_space=pl.ANY)],
+        in_specs=[pl.BlockSpec(memory_space=pl.ANY)],
         out_specs=[pl.BlockSpec(memory_space=pltpu.VMEM)] * len(shapes),
         out_shape=shapes,
         scratch_shapes=[pltpu.SemaphoreType.DMA((len(shapes) * cols,))],
         cost_estimate=cost(0, 8 * cols * slots * sum(widths)),
         name="cut_blocks",
-    )(starts, b_eval)
+    )(b_eval)
 
 
 def pack(blocks, select, at, w):
@@ -155,35 +156,33 @@
             crossings = [[part]]
         r = lax.axis_index("row")
 
-        starts = (jnp.arange(cols) * per + r * part).astype(jnp.int32)
-        cut = cut_blocks(b_eval, starts, [sum(c) for c in crossings])
+        cut = cut_blocks(b_eval, cols, rows, [sum(c) for c in crossings])
         a_whole = lax.all_gather(a_terms, "col", axis=0, tiled=True)
         used = term_slot[:, None] == jnp.arange(cols * slots)[None, :]
         select = jnp.where(used, term_sign[:, None], 0).astype(BF16)
         high, low = split_a([a_whole])
 
-        mine, places, pieces, offset, blocks = [], [], [], 0, None
-        for c, widths in enumerate(crossings):
-            block = cut[c] if blocks is None else after(cut[c], blocks)
-            blocks = lax.all_to_all(block, "col", 0, 0, tiled=True)
-            if c and c == len(crossings) - 1:
-                blocks = after(blocks, high, low)
-            at = 0
-            for w in widths:
-                mine.append(pack(blocks, select, at, w))
-                if rows == 4:
-                    pieces.append([mine[-1]] + [lax.ppermute(mine[-1], "row", [(q, q ^ n) for q in range(4)]) for n in (1, 2, 3)])
-                    quarter = jnp.stack([r, r ^ 1, r ^ 2, r ^ 3])
-                else:
-                    pieces.append(list(lax.all_gather(mine[-1], "row")))
-                    quarter = jnp.arange(rows)
-                places.append((quarter * (part // w) + offset // w).astype(jnp.int32))
-                at, offset = at + w, offset + w
-        joint = None
-        for n in range(len(mine)):
-            ready = pieces[n] if n == len(mine) - 1 else after(pieces[n], mine[n + 1])
-            joint = product(high, low, ready, places[n], joint, per)
-        return joint
+        crossed = []
+        for block in cut:
+            crossed.append(lax.all_to_all(after(block, crossed), "col", 0, 0, tiled=True))
+
+        if len(cut) == 1:
+            pieces = list(lax.all_gather(pack(crossed[0], select, 0, part), "row"))
+            return product(high, low, pieces, jnp.arange(rows, dtype=jnp.int32), None, per)
+
+        def share(x):
+            return [lax.ppermute(x, "row", [(q, q ^ way) for q in range(4)]) for way in (1, 2, 3)]
+
+        w = part // 2
+        quarter = (2 * jnp.stack([r, r ^ 1, r ^ 2, r ^ 3])).astype(jnp.int32)
+        first = pack(crossed[0], select, 0, w)
+        shared = share(first)
+        joint = product(high, low, [first], quarter[:1], None, per)
+        second = pack(after(crossed[1], joint), select, 0, w)
+        shared_second = share(second)
+        places = jnp.concatenate([quarter[1:], quarter[:1] + 1])
+        joint = product(high, low, after(shared, second) + [second], places, joint, per)
+        return product(high, low, shared_second, quarter[1:] + 1, joint, per)
 
     return jax.shard_map(
         shards,

time: 157 us -> 150 us (0.955)
  waiting for transfers between devices: 17 us -> 8.71 us
    all_to_all x1, waiting for transfers between devices: 14.8 us -> 6.51 us  [shards(): lax.all_to_all(after(block, crossed), 'col', 0, 0, tiled=True)]
    pallas_call x2 -> x3, Pallas kernels: 39.6 us -> 41.4 us  [product(): pl.pallas_call(kernel, grid_spec=pltpu.PrefetchScalarGridSpec(num_scalar_...]
    unnamed x10 -> x12, local copies, waits for them, and re-layouts: 2.38 us -> 3.45 us
  transfers between devices with their start and end apart: 8 -> 8, of which waited for: 3 -> 3; matrix products, arithmetic and copies ran while one was open for 1% -> 1% of each run, Pallas kernels for 20% -> 26%
where the time goes in v3:
time: 150 us; the launch traced here: 149 us
  blocking collectives  58.4 us (39%)
  Pallas kernels  53 us (35%)
  between operations  13.5 us (9%)
  starting transfers between devices  11.2 us (7%)
  waiting for transfers between devices  8.71 us (6%)
  local copies, waits for them, and re-layouts  3.45 us (2%)
    all_to_all x1, blocking collectives, shards(): lax.all_to_all(after(block, crossed), 'col', 0, 0, tiled=True)  58.4 us
    pallas_call x3, Pallas kernels, product(): pl.pallas_call(kernel, grid_spec=pltpu.PrefetchScalarGridSpec(num_scalar_...  41.4 us
    ppermute x6, starting transfers between devices, share(): lax.ppermute(x, 'row', [(q, q ^ way) for q in range(4)])  6.99 us
    all_to_all x1, waiting for transfers between devices, shards(): lax.all_to_all(after(block, crossed), 'col', 0, 0, tiled=True)  6.51 us
    pallas_call x2, Pallas kernels, pack(): pl.pallas_call(kernel, grid=(w // tile,), in_specs=[pl.BlockSpec(select.s...  4.91 us
    all_to_all x1, starting transfers between devices, shards(): lax.all_to_all(after(block, crossed), 'col', 0, 0, tiled=True)  4.25 us
    pallas_call x1, Pallas kernels, split_a(): pl.pallas_call(kernel, grid=(bins // tile,), in_specs=[pl.BlockSpec((held...  3.59 us
    unnamed x12, local copies, waits for them, and re-layouts  3.45 us
  transfers between devices with their start and end apart: 8, of which 3 were waited for; matrix products, arithmetic and copies ran while one was open for 1% of the time, Pallas kernels for 26%

profile of v3, /device:TPU:0, one launch (start us, length us, event | category | flops | bytes accessed | tf_op | source)
XLA Modules:
  0.0 149.4 jit_solution(16775090739754796140)
XLA Ops:
  6.5 0.0 copy-start.4
  6.5 0.0 copy-start.5
  6.5 0.0 all-gather.2.cloned.1.call-start
  6.5 0.7 all-gather.2.cloned.1.call-update
  7.3 3.1 %cut_blocks.1 = (f32[8,64,512]{2,1,0:T(8,128)}, f32[8,64,512]{2,1,0:T(8,128)}) custom-call(f32[64,32768]{1,0:T(8,128)} %b_ref.1), custom_call_target="tpu_custom_call" | custom-call | bytes 4194304 | tf_op jit(solution)/shard_map/cut_blocks/pallas_call | solution.py:46
  10.4 58.4 %all_to_all.10.block_ref = f32[8,64,512]{2,1,0:T(8,128)} all-to-all(f32[8,64,512]{2,1,0:T(8,128)} %get-tuple-element.17), channel_id=1, replica_groups=mesh['row'=4,'col'=8] {'col'}, dimensions={0} | all-to-all | bytes 2097152 | tf_op jit(solution)/shard_map/all_to_all | solution.py:167
  68.7 4.2 %all-to-all-start.1 = ((f32[8,64,512]{2,1,0:T(8,128)}), f32[8,64,512]{2,1,0:T(8,128)}, u32[]{:S(2)}, u32[]{:S(2)}) async-start(f32[8,64,512]{2,1,0:T(8,128)} %get-tuple-element.18), calls=%async_computation.1 | async-start | bytes 2097152 | tf_op jit(solution)/shard_map/all_to_all | solution.py:167
  73.0 0.1 add_multiply_fusion
  73.1 0.0 copy-done.4
  73.1 0.0 copy-done.5
  73.1 0.9 select_convert_fusion.select_ref
  74.0 2.5 %pack.2.refs_0_ = f32[256,512]{1,0:T(8,128)} custom-call(bf16[256,512]{1,0:T(8,128)(2,1)} %select_convert_fusion.select_ref, f32[8,64,512]{2,1,0:T(8,128)} %all_to_all.10.block_ref), custom_call_target="tpu_custom_call" | custom-call | flops 268435456 | bytes 1572864 | tf_op jit(solution)/shard_map/pack/pallas_call | solution.py:66
  76.4 2.5 %collective-permute-start.5 = (f32[256,512]{1,0:T(8,128)}, f32[256,512]{1,0:T(8,128)S(1)}, u32[]{:S(2)}, u32[]{:S(2)}) collective-permute-start(f32[256,512]{1,0:T(8,128)} %pack.2.refs_0_), channel_id=1, source_target_pairs={{0,24},{8,16},{16,8},{24,0},{1,25},{9,17},{17,9},{25,1},{2,26},{10... | collective-permute-start | bytes 1572872 | tf_op jit(solution)/shard_map/ppermute | solution.py:174
  78.9 0.5 collective-permute-start.4
  79.4 0.5 collective-permute-start.3
  79.9 0.1 fusion
  80.1 0.1 pad_add_fusion.places_ref
  80.1 0.0 all-gather.2.cloned.1.call-done.refs_0_
  80.1 3.6 %split_a.1 = (bf16[4096,256]{1,0:T(8,128)(2,1)S(1)}, bf16[4096,256]{1,0:T(8,128)(2,1)S(1)}) custom-call(f32[256,4096]{1,0:T(8,128)} %all-gather.2.cloned.1.call-done.refs_0_), custom_call_target="tpu_custom_call" | custom-call | bytes 8388608 | tf_op jit(solution)/shard_map/split_a/pallas_call | solution.py:90
  83.7 0.0 copy-start.2
  83.7 1.0 copy-done.2
  84.8 7.0 %product.3.refs_4_ = f32[4096,4096]{1,0:T(8,128)} custom-call(s32[1]{0:T(128)S(1)} %bitcast.6, bf16[4096,256]{1,0:T(8,128)(2,1)S(1)} %get-tuple-element.14.high_ref, bf16[4096,256]{1,0:T(8,128)(2,1)S(1)} %get-tuple-element.15.low_ref, f32[256,512]{1,0:T(8,128)S(1)} %copy-done.2), custom_call_target="tpu_custom_call" | custom-call | flops 3221225472 | bytes 8388608 | tf_op jit(solution)/shard_map/product/pallas_call | solution.py:123
  91.7 0.0 copy-start
  91.7 1.3 copy-done
  93.1 6.5 %all-to-all-done.1.block_ref = f32[8,64,512]{2,1,0:T(8,128)} async-done(((f32[8,64,512]{2,1,0:T(8,128)}), f32[8,64,512]{2,1,0:T(8,128)}, u32[]{:S(2)}, u32[]{:S(2)}) %all-to-all-start.1) | async-done | bytes 1048608 | tf_op jit(solution)/shard_map/all_to_all | solution.py:167
  99.6 2.4 %pack.3.refs_3_ = f32[256,512]{1,0:T(8,128)} custom-call(bf16[256,512]{1,0:T(8,128)(2,1)} %select_convert_fusion.select_ref, f32[8,64,512]{2,1,0:T(8,128)} %all-to-all-done.1.block_ref), custom_call_target="tpu_custom_call" | custom-call | flops 268435456 | bytes 1572864 | tf_op jit(solution)/shard_map/pack/pallas_call | solution.py:66
  102.0 0.0 copy-start.1
  102.0 2.5 %collective-permute-start.2 = (f32[256,512]{1,0:T(8,128)}, f32[256,512]{1,0:T(8,128)S(1)}, u32[]{:S(2)}, u32[]{:S(2)}) collective-permute-start(f32[256,512]{1,0:T(8,128)} %pack.3.refs_3_), channel_id=1, source_target_pairs={{0,24},{8,16},{16,8},{24,0},{1,25},{9,17},{17,9},{25,1},{2,26},{10... | collective-permute-start | bytes 1572872 | tf_op jit(solution)/shard_map/ppermute | solution.py:174
  104.5 0.5 collective-permute-start.1
  105.0 0.0 collective-permute-done.5.refs_2_
  105.0 0.5 collective-permute-start
  105.5 0.0 collective-permute-done.4.refs_1_
  105.5 0.0 collective-permute-done.3.refs_0_
  105.5 0.0 copy-start.3
  105.5 1.1 copy-done.3
  106.6 19.9 %product.4.refs_3_ = f32[4096,4096]{1,0:T(8,128)} custom-call(s32[4]{0:T(128)S(1)} %pad_add_fusion.places_ref, bf16[4096,256]{1,0:T(8,128)(2,1)S(1)} %get-tuple-element.14.high_ref, bf16[4096,256]{1,0:T(8,128)(2,1)} %copy-done, f32[256,512]{1,0:T(8,128)} %collective-permute-done.3.refs_0_, ...), custom_call_target="tpu_custom_call", output_to_operand_aliasing={{}: (7, {})} | custom-call | flops 12884901888 | bytes 33554432 | tf_op jit(solution)/shard_map/product/pallas_call | solution.py:123
  126.5 0.0 collective-permute-done.2.refs_2_
  126.5 1.4 collective-permute-done.1.refs_1_
  127.9 0.1 collective-permute-done.refs_0_
  128.0 0.0 copy-done.1
  128.0 14.6 %product.5 = f32[4096,4096]{1,0:T(8,128)} custom-call(s32[3]{0:T(128)S(1)} %get-tuple-element.24.places_ref, bf16[4096,256]{1,0:T(8,128)(2,1)S(1)} %get-tuple-element.14.high_ref, bf16[4096,256]{1,0:T(8,128)(2,1)S(1)} %copy-done.1, f32[256,512]{1,0:T(8,128)S(1)} %collective-permute-done.refs_0_, ...), custom_call_target="tpu_custom_call", output_to_operand_aliasing={{}: (6, {})} | custom-call | flops 9663676416 | bytes 25165824 | tf_op jit(solution)/shard_map/product/pallas_call | solution.py:123
Async XLA Ops:
  6.5 66.5 %copy-start.4 = (s32[256]{0:T(256)S(1)}, s32[256]{0:T(256)}, u32[]{:S(2)}) copy-start(s32[256]{0:T(256)} %param.7) | copy-start | bytes 3076
  6.5 66.5 %copy-start.5 = (s32[256]{0:T(256)S(1)}, s32[256]{0:T(256)}, u32[]{:S(2)}) copy-start(s32[256]{0:T(256)} %param.6) | copy-start | bytes 3076
  6.5 73.6 %all-gather.2.cloned.1.call-start = ((), (), s32[]{:S(2)}) async-start(), calls=%async_computation.2 | async-start | bytes 4718592 | tf_op jit(solution)/shard_map/all_gather | solution.py:160
  68.7 30.9 %all-to-all-start.1 = ((f32[8,64,512]{2,1,0:T(8,128)}), f32[8,64,512]{2,1,0:T(8,128)}, u32[]{:S(2)}, u32[]{:S(2)}) async-start(f32[8,64,512]{2,1,0:T(8,128)} %get-tuple-element.18), calls=%async_computation.1 | async-start | bytes 2097152 | tf_op jit(solution)/shard_map/all_to_all | solution.py:167
  76.4 28.6 %collective-permute-start.5 = (f32[256,512]{1,0:T(8,128)}, f32[256,512]{1,0:T(8,128)S(1)}, u32[]{:S(2)}, u32[]{:S(2)}) collective-permute-start(f32[256,512]{1,0:T(8,128)} %pack.2.refs_0_), channel_id=1, source_target_pairs={{0,24},{8,16},{16,8},{24,0},{1,25},{9,17},{17,9},{25,1},{2,26},{10... | collective-permute-start | bytes 1572872 | tf_op jit(solution)/shard_map/ppermute | solution.py:174
  78.9 26.6 %collective-permute-start.4 = (f32[256,512]{1,0:T(8,128)}, f32[256,512]{1,0:T(8,128)S(1)}, u32[]{:S(2)}, u32[]{:S(2)}) collective-permute-start(f32[256,512]{1,0:T(8,128)} %pack.2.refs_0_), channel_id=1, source_target_pairs={{0,16},{8,24},{16,0},{24,8},{1,17},{9,25},{17,1},{25,9},{2,18},{10... | collective-permute-start | bytes 1572872 | tf_op jit(solution)/shard_map/ppermute | solution.py:174
  79.4 26.1 %collective-permute-start.3 = (f32[256,512]{1,0:T(8,128)}, f32[256,512]{1,0:T(8,128)}, u32[]{:S(2)}, u32[]{:S(2)}) collective-permute-start(f32[256,512]{1,0:T(8,128)} %pack.2.refs_0_), channel_id=1, source_target_pairs={{0,8},{8,0},{16,24},{24,16},{1,9},{9,1},{17,25},{25,17},{2,10},{10... | collective-permute-start | bytes 1572872 | tf_op jit(solution)/shard_map/ppermute | solution.py:174
  83.7 1.0 copy-start.2
  91.7 1.3 copy-start
  102.0 25.9 %copy-start.1 = (bf16[4096,256]{1,0:T(8,128)(2,1)S(1)}, bf16[4096,256]{1,0:T(8,128)(2,1)}, u32[]{:S(2)}) copy-start(bf16[4096,256]{1,0:T(8,128)(2,1)} %copy-done) | copy-start | bytes 6291460
  102.0 24.4 %collective-permute-start.2 = (f32[256,512]{1,0:T(8,128)}, f32[256,512]{1,0:T(8,128)S(1)}, u32[]{:S(2)}, u32[]{:S(2)}) collective-permute-start(f32[256,512]{1,0:T(8,128)} %pack.3.refs_3_), channel_id=1, source_target_pairs={{0,24},{8,16},{16,8},{24,0},{1,25},{9,17},{17,9},{25,1},{2,26},{10... | collective-permute-start | bytes 1572872 | tf_op jit(solution)/shard_map/ppermute | solution.py:174
  104.5 23.4 %collective-permute-start.1 = (f32[256,512]{1,0:T(8,128)}, f32[256,512]{1,0:T(8,128)S(1)}, u32[]{:S(2)}, u32[]{:S(2)}) collective-permute-start(f32[256,512]{1,0:T(8,128)} %pack.3.refs_3_), channel_id=1, source_target_pairs={{0,16},{8,24},{16,0},{24,8},{1,17},{9,25},{17,1},{25,9},{2,18},{10... | collective-permute-start | bytes 1572872 | tf_op jit(solution)/shard_map/ppermute | solution.py:174
  105.0 23.0 %collective-permute-start = (f32[256,512]{1,0:T(8,128)}, f32[256,512]{1,0:T(8,128)S(1)}, u32[]{:S(2)}, u32[]{:S(2)}) collective-permute-start(f32[256,512]{1,0:T(8,128)} %pack.3.refs_3_), channel_id=1, source_target_pairs={{0,8},{8,0},{16,24},{24,16},{1,9},{9,1},{17,25},{25,17},{2,10},{10... | collective-permute-start | bytes 1572872 | tf_op jit(solution)/shard_map/ppermute | solution.py:174
  105.5 1.1 copy-start.3
Sparse Core Ops, SparseCore 0:
  9.0 69.6 all-gather.1

commit v4 on v3

--- a/solution.py
+++ b/solution.py
@@ -22,7 +22,7 @@
     return pl.CostEstimate(flops=flops, bytes_accessed=moved, transcendentals=0)
 
 
-def cut_blocks(b_eval, cols, rows, widths):
+def cut_blocks(b_eval, cols, rows, widths, begin=0):
     slots, per = b_eval.shape[0], b_eval.shape[1] // cols
     shapes = [jax.ShapeDtypeStruct((cols, slots, w), F32) for w in widths]
 
@@ -30,7 +30,7 @@
         mine = lax.axis_index("row") * (per // rows)
         outs, sems = refs[:-1], refs[-1]
         copies = []
-        offset = 0
+        offset = begin
         for chunk, w in enumerate(widths):
             for q in range(cols):
                 start = pl.multiple_of(mine + (q * per + offset), 128)
@@ -156,7 +156,7 @@
             crossings = [[part]]
         r = lax.axis_index("row")
 
-        cut = cut_blocks(b_eval, cols, rows, [sum(c) for c in crossings])
+        cut = [cut_blocks(b_eval, cols, rows, [part // len(crossings)], n * part // len(crossings))[0] for n in range(len(crossings))]
         a_whole = lax.all_gather(a_terms, "col", axis=0, tiled=True)
         used = term_slot[:, None] == jnp.arange(cols * slots)[None, :]
         select = jnp.where(used, term_sign[:, None], 0).astype(BF16)

time: 150 us -> 150 us (level)
  blocking collectives: 58.4 us -> 0 us
  waiting for transfers between devices: 8.71 us -> 58.8 us
  starting transfers between devices: 11.2 us -> 17.6 us
  Pallas kernels: 53 us -> 54.6 us
    all_to_all x1 -> x0, blocking collectives: 58.4 us -> none  [shards(): lax.all_to_all(after(block, crossed), 'col', 0, 0, tiled=True)]
    all_to_all x1 -> x2, waiting for transfers between devices: 6.51 us -> 56.4 us  [shards(): lax.all_to_all(after(block, crossed), 'col', 0, 0, tiled=True)]
    all_to_all x1 -> x2, starting transfers between devices: 4.25 us -> 10.6 us  [shards(): lax.all_to_all(after(block, crossed), 'col', 0, 0, tiled=True)]
    pallas_call x1 -> x2, Pallas kernels: 3.11 us -> 4.67 us  [cut_blocks(): pl.pallas_call(kernel, in_specs=[pl.BlockSpec(memory_space=pl.ANY)], out_...]
    unnamed x12 -> x14, local copies, waits for them, and re-layouts: 3.45 us -> 3.45 us
  transfers between devices with their start and end apart: 8 -> 9, of which waited for: 3 -> 4; matrix products, arithmetic and copies ran while one was open for 1% -> 1% of each run, Pallas kernels for 26% -> 27%
where the time goes in v4:
time: 150 us; the launch traced here: 149 us
  waiting for transfers between devices  58.8 us (39%)
  Pallas kernels  54.6 us (36%)
  starting transfers between devices  17.6 us (12%)
  between operations  13.5 us (9%)
  local copies, waits for them, and re-layouts  3.45 us (2%)
    all_to_all x2, waiting for transfers between devices, shards(): lax.all_to_all(after(block, crossed), 'col', 0, 0, tiled=True)  56.4 us
    pallas_call x3, Pallas kernels, product(): pl.pallas_call(kernel, grid_spec=pltpu.PrefetchScalarGridSpec(num_scalar_...  41.4 us
    all_to_all x2, starting transfers between devices, shards(): lax.all_to_all(after(block, crossed), 'col', 0, 0, tiled=True)  10.6 us
    ppermute x6, starting transfers between devices, share(): lax.ppermute(x, 'row', [(q, q ^ way) for q in range(4)])  6.99 us
    pallas_call x2, Pallas kernels, pack(): pl.pallas_call(kernel, grid=(w // tile,), in_specs=[pl.BlockSpec(select.s...  4.96 us
    pallas_call x2, Pallas kernels, cut_blocks(): pl.pallas_call(kernel, in_specs=[pl.BlockSpec(memory_space=pl.ANY)], out_...  4.67 us
    pallas_call x1, Pallas kernels, split_a(): pl.pallas_call(kernel, grid=(bins // tile,), in_specs=[pl.BlockSpec((held...  3.59 us
    unnamed x14, local copies, waits for them, and re-layouts  3.45 us
  transfers between devices with their start and end apart: 9, of which 4 were waited for; matrix products, arithmetic and copies ran while one was open for 1% of the time, Pallas kernels for 27%

profile of v4, /device:TPU:0, one launch (start us, length us, event | category | flops | bytes accessed | tf_op | source)
XLA Modules:
  0.0 149.0 jit_solution(17445494227998876556)
XLA Ops:
  6.5 0.0 all-gather.2.cloned.1.call-start
  6.5 0.7 all-gather.2.cloned.1.call-update
  7.3 2.3 %cut_blocks.3 = f32[8,64,512]{2,1,0:T(8,128)} custom-call(f32[64,32768]{1,0:T(8,128)} %b_ref.3), custom_call_target="tpu_custom_call" | custom-call | bytes 2097152 | tf_op jit(solution)/shard_map/cut_blocks/pallas_call | solution.py:46
  9.6 0.0 copy-start.5
  9.6 0.0 copy-start.6
  9.6 6.3 %all-to-all-start = ((f32[8,64,512]{2,1,0:T(8,128)}), f32[8,64,512]{2,1,0:T(8,128)S(1)}, u32[]{:S(2)}, u32[]{:S(2)}) async-start(f32[8,64,512]{2,1,0:T(8,128)} %cut_blocks.3), calls=%async_computation | async-start | bytes 2097152 | tf_op jit(solution)/shard_map/all_to_all | solution.py:167
  16.0 2.3 %cut_blocks.2 = f32[8,64,512]{2,1,0:T(8,128)} custom-call(f32[64,32768]{1,0:T(8,128)} %b_ref.3), custom_call_target="tpu_custom_call" | custom-call | bytes 2097152 | tf_op jit(solution)/shard_map/cut_blocks/pallas_call | solution.py:46
  18.3 49.6 %all-to-all-done.block_ref = f32[8,64,512]{2,1,0:T(8,128)S(1)} async-done(((f32[8,64,512]{2,1,0:T(8,128)}), f32[8,64,512]{2,1,0:T(8,128)S(1)}, u32[]{:S(2)}, u32[]{:S(2)}) %all-to-all-start) | async-done | bytes 1048608 | tf_op jit(solution)/shard_map/all_to_all | solution.py:167
  67.9 0.0 copy-start.4
  67.9 4.2 %all-to-all-start.1 = ((f32[8,64,512]{2,1,0:T(8,128)}), f32[8,64,512]{2,1,0:T(8,128)}, u32[]{:S(2)}, u32[]{:S(2)}) async-start(f32[8,64,512]{2,1,0:T(8,128)} %cut_blocks.2), calls=%async_computation.1 | async-start | bytes 2097152 | tf_op jit(solution)/shard_map/all_to_all | solution.py:167
  72.1 0.1 add_multiply_fusion
  72.2 0.0 copy-done.5
  72.2 0.0 copy-done.6
  72.2 0.8 select_convert_fusion.select_ref
  73.1 0.0 copy-done.4
  73.1 2.5 %pack.2.refs_0_ = f32[256,512]{1,0:T(8,128)} custom-call(bf16[256,512]{1,0:T(8,128)(2,1)} %select_convert_fusion.select_ref, f32[8,64,512]{2,1,0:T(8,128)} %copy-done.4), custom_call_target="tpu_custom_call" | custom-call | flops 268435456 | bytes 1572864 | tf_op jit(solution)/shard_map/pack/pallas_call | solution.py:66
  75.5 2.5 %collective-permute-start.5 = (f32[256,512]{1,0:T(8,128)}, f32[256,512]{1,0:T(8,128)S(1)}, u32[]{:S(2)}, u32[]{:S(2)}) collective-permute-start(f32[256,512]{1,0:T(8,128)} %pack.2.refs_0_), channel_id=1, source_target_pairs={{0,24},{8,16},{16,8},{24,0},{1,25},{9,17},{17,9},{25,1},{2,26},{10... | collective-permute-start | bytes 1572872 | tf_op jit(solution)/shard_map/ppermute | solution.py:174
  78.0 0.5 collective-permute-start.4
  78.5 0.5 collective-permute-start.3
  79.0 0.1 fusion
  79.1 0.1 pad_add_fusion.places_ref
  79.2 0.0 all-gather.2.cloned.1.call-done.refs_0_
  79.2 3.6 %split_a.1 = (bf16[4096,256]{1,0:T(8,128)(2,1)S(1)}, bf16[4096,256]{1,0:T(8,128)(2,1)S(1)}) custom-call(f32[256,4096]{1,0:T(8,128)} %all-gather.2.cloned.1.call-done.refs_0_), custom_call_target="tpu_custom_call" | custom-call | bytes 8388608 | tf_op jit(solution)/shard_map/split_a/pallas_call | solution.py:90
  82.8 0.0 copy-start.2
  82.8 1.0 copy-done.2
  83.9 7.0 %product.3.refs_4_ = f32[4096,4096]{1,0:T(8,128)} custom-call(s32[1]{0:T(128)S(1)} %bitcast.6, bf16[4096,256]{1,0:T(8,128)(2,1)S(1)} %get-tuple-element.12.high_ref, bf16[4096,256]{1,0:T(8,128)(2,1)S(1)} %get-tuple-element.13.low_ref, f32[256,512]{1,0:T(8,128)S(1)} %copy-done.2), custom_call_target="tpu_custom_call" | custom-call | flops 3221225472 | bytes 8388608 | tf_op jit(solution)/shard_map/product/pallas_call | solution.py:123
  90.8 0.0 copy-start
  90.8 1.3 copy-done
  92.2 6.8 %all-to-all-done.1.block_ref = f32[8,64,512]{2,1,0:T(8,128)} async-done(((f32[8,64,512]{2,1,0:T(8,128)}), f32[8,64,512]{2,1,0:T(8,128)}, u32[]{:S(2)}, u32[]{:S(2)}) %all-to-all-start.1) | async-done | bytes 1048608 | tf_op jit(solution)/shard_map/all_to_all | solution.py:167
  99.0 2.5 %pack.3.refs_3_ = f32[256,512]{1,0:T(8,128)} custom-call(bf16[256,512]{1,0:T(8,128)(2,1)} %select_convert_fusion.select_ref, f32[8,64,512]{2,1,0:T(8,128)} %all-to-all-done.1.block_ref), custom_call_target="tpu_custom_call" | custom-call | flops 268435456 | bytes 1572864 | tf_op jit(solution)/shard_map/pack/pallas_call | solution.py:66
  101.5 0.0 copy-start.1
  101.5 2.5 %collective-permute-start.2 = (f32[256,512]{1,0:T(8,128)}, f32[256,512]{1,0:T(8,128)S(1)}, u32[]{:S(2)}, u32[]{:S(2)}) collective-permute-start(f32[256,512]{1,0:T(8,128)} %pack.3.refs_3_), channel_id=1, source_target_pairs={{0,24},{8,16},{16,8},{24,0},{1,25},{9,17},{17,9},{25,1},{2,26},{10... | collective-permute-start | bytes 1572872 | tf_op jit(solution)/shard_map/ppermute | solution.py:174
  103.9 0.5 collective-permute-start.1
  104.4 0.0 collective-permute-done.5.refs_2_
  104.4 0.5 collective-permute-start
  105.0 0.0 collective-permute-done.4.refs_1_
  105.0 0.0 collective-permute-done.3.refs_0_
  105.0 0.0 copy-start.3
  105.0 1.1 copy-done.3
  106.0 19.9 %product.4.refs_3_ = f32[4096,4096]{1,0:T(8,128)} custom-call(s32[4]{0:T(128)S(1)} %pad_add_fusion.places_ref, bf16[4096,256]{1,0:T(8,128)(2,1)S(1)} %get-tuple-element.12.high_ref, bf16[4096,256]{1,0:T(8,128)(2,1)} %copy-done, f32[256,512]{1,0:T(8,128)} %collective-permute-done.3.refs_0_, ...), custom_call_target="tpu_custom_call", output_to_operand_aliasing={{}: (7, {})} | custom-call | flops 12884901888 | bytes 33554432 | tf_op jit(solution)/shard_map/product/pallas_call | solution.py:123
  125.9 0.0 collective-permute-done.2.refs_2_
  125.9 1.6 %collective-permute-done.1.refs_1_ = f32[256,512]{1,0:T(8,128)S(1)} collective-permute-done((f32[256,512]{1,0:T(8,128)}, f32[256,512]{1,0:T(8,128)S(1)}, u32[]{:S(2)}, u32[]{:S(2)}) %collective-permute-start.1) | collective-permute-done | bytes 524320 | tf_op jit(solution)/shard_map/ppermute | solution.py:174
  127.5 0.1 collective-permute-done.refs_0_
  127.5 0.0 copy-done.1
  127.5 14.6 %product.5 = f32[4096,4096]{1,0:T(8,128)} custom-call(s32[3]{0:T(128)S(1)} %get-tuple-element.20.places_ref, bf16[4096,256]{1,0:T(8,128)(2,1)S(1)} %get-tuple-element.12.high_ref, bf16[4096,256]{1,0:T(8,128)(2,1)S(1)} %copy-done.1, f32[256,512]{1,0:T(8,128)S(1)} %collective-permute-done.refs_0_, ...), custom_call_target="tpu_custom_call", output_to_operand_aliasing={{}: (6, {})} | custom-call | flops 9663676416 | bytes 25165824 | tf_op jit(solution)/shard_map/product/pallas_call | solution.py:123
Async XLA Ops:
  6.5 72.7 %all-gather.2.cloned.1.call-start = ((), (), s32[]{:S(2)}) async-start(), calls=%async_computation.2 | async-start | bytes 4718592 | tf_op jit(solution)/shard_map/all_gather | solution.py:160
  9.6 62.6 %copy-start.5 = (s32[256]{0:T(256)S(1)}, s32[256]{0:T(256)}, u32[]{:S(2)}) copy-start(s32[256]{0:T(256)} %param.7) | copy-start | bytes 3076
  9.6 62.6 %copy-start.6 = (s32[256]{0:T(256)S(1)}, s32[256]{0:T(256)}, u32[]{:S(2)}) copy-start(s32[256]{0:T(256)} %param.6) | copy-start | bytes 3076
  9.6 58.3 %all-to-all-start = ((f32[8,64,512]{2,1,0:T(8,128)}), f32[8,64,512]{2,1,0:T(8,128)S(1)}, u32[]{:S(2)}, u32[]{:S(2)}) async-start(f32[8,64,512]{2,1,0:T(8,128)} %cut_blocks.3), calls=%async_computation | async-start | bytes 2097152 | tf_op jit(solution)/shard_map/all_to_all | solution.py:167
  67.9 5.2 %copy-start.4 = (f32[8,64,512]{2,1,0:T(8,128)}, f32[8,64,512]{2,1,0:T(8,128)S(1)}, u32[]{:S(2)}) copy-start(f32[8,64,512]{2,1,0:T(8,128)S(1)} %all-to-all-done.block_ref) | copy-start | bytes 3145732
  67.9 31.1 %all-to-all-start.1 = ((f32[8,64,512]{2,1,0:T(8,128)}), f32[8,64,512]{2,1,0:T(8,128)}, u32[]{:S(2)}, u32[]{:S(2)}) async-start(f32[8,64,512]{2,1,0:T(8,128)} %cut_blocks.2), calls=%async_computation.1 | async-start | bytes 2097152 | tf_op jit(solution)/shard_map/all_to_all | solution.py:167
  75.5 28.9 %collective-permute-start.5 = (f32[256,512]{1,0:T(8,128)}, f32[256,512]{1,0:T(8,128)S(1)}, u32[]{:S(2)}, u32[]{:S(2)}) collective-permute-start(f32[256,512]{1,0:T(8,128)} %pack.2.refs_0_), channel_id=1, source_target_pairs={{0,24},{8,16},{16,8},{24,0},{1,25},{9,17},{17,9},{25,1},{2,26},{10... | collective-permute-start | bytes 1572872 | tf_op jit(solution)/shard_map/ppermute | solution.py:174
  78.0 26.9 %collective-permute-start.4 = (f32[256,512]{1,0:T(8,128)}, f32[256,512]{1,0:T(8,128)S(1)}, u32[]{:S(2)}, u32[]{:S(2)}) collective-permute-start(f32[256,512]{1,0:T(8,128)} %pack.2.refs_0_), channel_id=1, source_target_pairs={{0,16},{8,24},{16,0},{24,8},{1,17},{9,25},{17,1},{25,9},{2,18},{10... | collective-permute-start | bytes 1572872 | tf_op jit(solution)/shard_map/ppermute | solution.py:174
  78.5 26.5 %collective-permute-start.3 = (f32[256,512]{1,0:T(8,128)}, f32[256,512]{1,0:T(8,128)}, u32[]{:S(2)}, u32[]{:S(2)}) collective-permute-start(f32[256,512]{1,0:T(8,128)} %pack.2.refs_0_), channel_id=1, source_target_pairs={{0,8},{8,0},{16,24},{24,16},{1,9},{9,1},{17,25},{25,17},{2,10},{10... | collective-permute-start | bytes 1572872 | tf_op jit(solution)/shard_map/ppermute | solution.py:174
  82.8 1.0 copy-start.2
  90.8 1.3 copy-start
  101.5 26.1 %copy-start.1 = (bf16[4096,256]{1,0:T(8,128)(2,1)S(1)}, bf16[4096,256]{1,0:T(8,128)(2,1)}, u32[]{:S(2)}) copy-start(bf16[4096,256]{1,0:T(8,128)(2,1)} %copy-done) | copy-start | bytes 6291460
  101.5 24.4 %collective-permute-start.2 = (f32[256,512]{1,0:T(8,128)}, f32[256,512]{1,0:T(8,128)S(1)}, u32[]{:S(2)}, u32[]{:S(2)}) collective-permute-start(f32[256,512]{1,0:T(8,128)} %pack.3.refs_3_), channel_id=1, source_target_pairs={{0,24},{8,16},{16,8},{24,0},{1,25},{9,17},{17,9},{25,1},{2,26},{10... | collective-permute-start | bytes 1572872 | tf_op jit(solution)/shard_map/ppermute | solution.py:174
  103.9 23.5 %collective-permute-start.1 = (f32[256,512]{1,0:T(8,128)}, f32[256,512]{1,0:T(8,128)S(1)}, u32[]{:S(2)}, u32[]{:S(2)}) collective-permute-start(f32[256,512]{1,0:T(8,128)} %pack.3.refs_3_), channel_id=1, source_target_pairs={{0,16},{8,24},{16,0},{24,8},{1,17},{9,25},{17,1},{25,9},{2,18},{10... | collective-permute-start | bytes 1572872 | tf_op jit(solution)/shard_map/ppermute | solution.py:174
  104.4 23.1 %collective-permute-start = (f32[256,512]{1,0:T(8,128)}, f32[256,512]{1,0:T(8,128)S(1)}, u32[]{:S(2)}, u32[]{:S(2)}) collective-permute-start(f32[256,512]{1,0:T(8,128)} %pack.3.refs_3_), channel_id=1, source_target_pairs={{0,8},{8,0},{16,24},{24,16},{1,9},{9,1},{17,25},{25,17},{2,10},{10... | collective-permute-start | bytes 1572872 | tf_op jit(solution)/shard_map/ppermute | solution.py:174
  105.0 1.1 copy-start.3
Sparse Core Ops, SparseCore 0:
  9.0 69.2 all-gather.1
